TPU v7x, 32 devices: a whole 2x2x4 slice. The times are simulated.
32 devices in a mesh: seq: 8 (over z, y), dp: 4 (over x, core).
Axes of the slice: x: 2, y: 2, z: 4, core: 2. Of those that a mesh axis runs over, the one named last changes fastest.
Arguments:
- block_input: bfloat16 [4, 1024, 1536], P('dp', 'seq'), may hold values from -6 to 6
- query_proj: bfloat16 [4, 1024, 768], P('dp', 'seq'), may hold values from -8 to 8
- key_proj: bfloat16 [4, 1024, 768], P('dp', 'seq'), may hold values from -8 to 8
- value_proj: bfloat16 [4, 1024, 768], P('dp', 'seq'), may hold values from -6 to 6
- lengths: int32 [4], P('dp'), may hold values from 256 to 1024, as said below
- out_proj: bfloat16 [1536, 768], replicated, may hold values from -0.21875 to 0.21875
- kernel: float32 [31, 1536], replicated, may hold values from -1 to 1
- conv_bias: float32 [1536], replicated, may hold values from -3 to 3
- grad_output: bfloat16 [4, 1024, 1536], P('dp', 'seq'), may hold values from -6 to 6
Outputs:
- block_output: bfloat16 [4, 1024, 1536], P('dp', 'seq')
- grad_input: bfloat16 [4, 1024, 1536], P('dp', 'seq')
- grad_query: bfloat16 [4, 1024, 768], P('dp', 'seq')
- grad_out_proj: float32 [1536, 768], P('seq')
- grad_kernel: float32 [31, 1536], P(None, 'seq')
- grad_bias: float32 [1536], P('seq')
Inputs may be any that keep to these rules, and one draw needn't show every extreme that they name: `lengths`: frames at or after an utterance's length are padding; in every draw at least one utterance has all 1024 frames valid.
All inputs are finite; a program needn't handle non-finite values.
Results may differ from a plain program's by a relative error of at most 0.012.
The roundings to bfloat16 on the way count: a program that leaves them out, or rounds other values in their place, can miss the bound.
Values may be sent and summed in bfloat16 or wider, within the bound.
No kernel may reach another device: no remote copies, remote signals or barrier semaphores. Data moves between devices by JAX's collectives and lax.ppermute only.
A program may use at most 128 MiB of HBM per device.

v0:
```python
import math
import jax
import jax.numpy as jnp
from jax import lax
from jax.sharding import PartitionSpec as P

D = 1536
H = 8
HS = 96
KW = 31
HD = 768


def with_halo(x, sides, width):
    for axis, dim in sides:
        size, length = (lax.axis_size(axis), x.shape[dim])
        up = [(i, (i + 1) % size) for i in range(size - 1)]
        down = [(j, i) for i, j in up]
        last = lax.slice_in_dim(x, length - width, length, axis=dim)
        leading = lax.slice_in_dim(x, 0, width, axis=dim)
        before = lax.ppermute(last, axis, up)
        after = lax.ppermute(leading, axis, down)
        x = jnp.concatenate([before, x, after], axis=dim)
    return x


def forward_rows(query_one, key_one, value_one, key_valid, score_scale):
    row_total = query_one.shape[0]
    block_rows = math.gcd(row_total, 512)
    query_blocks = query_one.reshape(row_total // block_rows, block_rows, query_one.shape[1])

    def forward_one_block(query_block):
        scores = (
            lax.dot_general(
                query_block, key_one, (((1,), (1,)), ((), ())), preferred_element_type=jnp.float32
            )
            * score_scale
        )
        scores = jnp.where(key_valid[None, :], scores, -jnp.inf)
        row_top = jnp.max(scores, axis=-1, keepdims=True)
        log_total = row_top + jnp.log(jnp.sum(jnp.exp(scores - row_top), axis=-1, keepdims=True))
        weights = jnp.exp(scores - log_total).astype(jnp.bfloat16)
        return (jnp.dot(weights, value_one, preferred_element_type=jnp.float32), log_total[:, 0])

    outputs, log_totals = lax.map(forward_one_block, query_blocks)
    return (outputs.reshape(row_total, query_one.shape[1]), log_totals.reshape(row_total))


def backward_rows(
    query_one, key_one, value_one, grad_one, lse_one, delta_one, key_valid, score_scale
):
    row_total = query_one.shape[0]
    block_rows = math.gcd(row_total, 512)
    block_count = row_total // block_rows
    width = query_one.shape[1]

    def backward_one_block(items):
        query_block, grad_block, lse_block, delta_block = items
        scores = (
            lax.dot_general(
                query_block, key_one, (((1,), (1,)), ((), ())), preferred_element_type=jnp.float32
            )
            * score_scale
        )
        scores = jnp.where(key_valid[None, :], scores, -jnp.inf)
        probs = jnp.exp(scores - lse_block[:, None])
        grad_prob = lax.dot_general(
            grad_block, value_one, (((1,), (1,)), ((), ())), preferred_element_type=jnp.float32
        )
        grad_score = (probs * (grad_prob - delta_block[:, None])).astype(jnp.bfloat16)
        return jnp.dot(grad_score, key_one, preferred_element_type=jnp.float32) * score_scale

    results = lax.map(
        backward_one_block,
        (
            query_one.reshape(block_count, block_rows, width),
            grad_one.reshape(block_count, block_rows, width),
            lse_one.reshape(block_count, block_rows),
            delta_one.reshape(block_count, block_rows),
        ),
    )
    return results.reshape(row_total, width)


def on_device(
    block_input, query_proj, key_proj, value_proj, lengths, out_proj, kernel, conv_bias, grad_output
):
    frames_dev = block_input.shape[1]
    seq_count = lax.axis_size("seq")
    total_frames = frames_dev * seq_count
    first_frame = lax.axis_index("seq") * frames_dev
    utt_length = lengths[0]
    local_valid = first_frame + jnp.arange(frames_dev) < utt_length
    all_valid = jnp.arange(total_frames) < utt_length
    score_scale = 1.0 / math.sqrt(HS)
    halo_width = KW // 2
    group_size = seq_count // H
    sub_rows = frames_dev // group_size
    query_local = query_proj[0]

    def to_serving(matrix):
        return matrix.reshape(frames_dev, H, HS).transpose(1, 0, 2).reshape(seq_count, sub_rows, HS)

    def from_serving(returned):
        return returned.reshape(H, frames_dev, HS).transpose(1, 0, 2).reshape(frames_dev, HD)

    query_mine = lax.all_to_all(
        to_serving(query_local), "seq", split_axis=0, concat_axis=1, tiled=True
    )[0]
    key_send = jnp.repeat(
        key_proj[0].reshape(frames_dev, H, HS).transpose(1, 0, 2), group_size, axis=0
    )
    value_send = jnp.repeat(
        value_proj[0].reshape(frames_dev, H, HS).transpose(1, 0, 2), group_size, axis=0
    )
    key_mine, value_mine = (
        lax.all_to_all(key_send, "seq", split_axis=0, concat_axis=1, tiled=True),
        lax.all_to_all(value_send, "seq", split_axis=0, concat_axis=1, tiled=True),
    )
    key_mine = key_mine[0]
    value_mine = value_mine[0]
    head_out, head_lse = forward_rows(query_mine, key_mine, value_mine, all_valid, score_scale)
    head_attended = head_out.astype(jnp.bfloat16)
    attended = from_serving(
        lax.all_to_all(head_attended[None], "seq", split_axis=1, concat_axis=0, tiled=True)
    )
    projected = lax.dot_general(
        attended, out_proj, (((1,), (1,)), ((), ())), preferred_element_type=jnp.float32
    )
    mixed_rows = (block_input[0].astype(jnp.float32) + projected).astype(jnp.bfloat16)
    masked = jnp.where(local_valid[:, None], mixed_rows, jnp.zeros_like(mixed_rows))
    padded = with_halo(masked, (("seq", 0),), halo_width).astype(jnp.float32)
    conv_rows = jnp.broadcast_to(conv_bias, (frames_dev, D))
    for tap in range(KW):
        conv_rows = conv_rows + kernel[tap] * padded[tap : tap + frames_dev]
    gate_rows = jax.nn.sigmoid(conv_rows)
    block_output = jnp.where(
        local_valid[:, None], mixed_rows.astype(jnp.float32) + conv_rows * gate_rows, 0.0
    ).astype(jnp.bfloat16)
    grad_rows = jnp.where(local_valid[:, None], grad_output[0].astype(jnp.float32), 0.0)
    grad_conv = grad_rows * gate_rows * (1.0 + conv_rows * (1.0 - gate_rows))
    kernel_local = jnp.stack(
        [jnp.sum(grad_conv * padded[tap : tap + frames_dev], axis=0) for tap in range(KW)]
    )
    bias_local = jnp.sum(grad_conv, axis=0)
    grad_padded = with_halo(grad_conv, (("seq", 0),), halo_width)
    grad_masked = jnp.zeros((frames_dev, D), jnp.float32)
    for tap in range(KW):
        begin = 2 * halo_width - tap
        grad_masked = grad_masked + kernel[tap] * grad_padded[begin : begin + frames_dev]
    grad_input = (grad_rows + jnp.where(local_valid[:, None], grad_masked, 0.0)).astype(
        jnp.bfloat16
    )
    grad_attn = jnp.dot(grad_input, out_proj, preferred_element_type=jnp.float32).astype(
        jnp.bfloat16
    )
    grad_mine = lax.all_to_all(
        to_serving(grad_attn), "seq", split_axis=0, concat_axis=1, tiled=True
    )[0]
    delta_mine = jnp.sum(grad_mine.astype(jnp.float32) * head_attended.astype(jnp.float32), axis=-1)
    grad_q_mine = backward_rows(
        query_mine, key_mine, value_mine, grad_mine, head_lse, delta_mine, all_valid, score_scale
    ).astype(jnp.bfloat16)
    grad_query = from_serving(
        lax.all_to_all(grad_q_mine[None], "seq", split_axis=1, concat_axis=0, tiled=True)
    )
    term_block = lax.dot_general(
        grad_input, attended, (((0,), (0,)), ((), ())), preferred_element_type=jnp.float32
    )
    partial_rows = lax.psum_scatter(term_block, "seq", scatter_dimension=0, tiled=True)
    summed = lax.psum(partial_rows.astype(jnp.bfloat16), "dp").astype(jnp.float32)
    kernel_total, bias_total = lax.psum((kernel_local, bias_local), ("seq", "dp"))
    shard_width = D // seq_count
    offset = lax.axis_index("seq") * shard_width
    grad_kernel = lax.dynamic_slice_in_dim(kernel_total, offset, shard_width, 1)
    grad_bias = lax.dynamic_slice_in_dim(bias_total, offset, shard_width, 0)
    return (block_output[None], grad_input[None], grad_query[None], summed, grad_kernel, grad_bias)


def solution(mesh):
    placed = (
        P("dp", "seq", None),
        P("dp", "seq", None),
        P("dp", "seq", None),
        P("dp", "seq", None),
        P("dp"),
        P(),
        P(),
        P(),
        P("dp", "seq", None),
    )
    return jax.shard_map(
        on_device,
        mesh=mesh,
        in_specs=placed,
        out_specs=(
            P("dp", "seq", None),
            P("dp", "seq", None),
            P("dp", "seq", None),
            P("seq", None),
            P(None, "seq"),
            P("seq"),
        ),
        check_vma=False,
    )
```

profile of v0, /device:TPU:0, one launch (start us, length us, event | category | flops | bytes accessed | tf_op | source)
XLA Modules:
  0.0 321.5 jit_solution(12944451114000263372)
XLA Ops:
  8.0 1.9 copy.76
  9.9 7.3 %all-to-all-start = ((bf16[8,128,96]{1,2,0:T(8,128)(2,1)}), bf16[8,128,96]{1,2,0:T(8,128)(2,1)S(1)}, u32[]{:S(2)}, u32[]{:S(2)}) async-start(bf16[8,128,96]{1,2,0:T(8,128)(2,1)} %bitcast.3), calls=%async_computation | async-start | bytes 393216 | tf_op jit(solution)/shard_map/all_to_all | solution.py:107
  17.2 1.7 copy.78
  18.9 6.2 %all-to-all-done = bf16[8,128,96]{1,2,0:T(8,128)(2,1)S(1)} async-done(((bf16[8,128,96]{1,2,0:T(8,128)(2,1)}), bf16[8,128,96]{1,2,0:T(8,128)(2,1)S(1)}, u32[]{:S(2)}, u32[]{:S(2)}) %all-to-all-start) | async-done | bytes 196640 | tf_op jit(solution)/shard_map/all_to_all | solution.py:107
  25.1 3.4 %all-to-all-start.1 = ((bf16[8,128,96]{1,2,0:T(8,128)(2,1)}), bf16[8,128,96]{1,2,0:T(8,128)(2,1)S(1)}, u32[]{:S(2)}, u32[]{:S(2)}) async-start(bf16[8,128,96]{1,2,0:T(8,128)(2,1)} %bitcast.5), calls=%async_computation.1 | async-start | bytes 393216 | tf_op jit(solution)/shard_map/all_to_all | solution.py:117
  28.5 1.7 copy.80
  30.3 6.0 %all-to-all-done.1 = bf16[8,128,96]{1,2,0:T(8,128)(2,1)S(1)} async-done(((bf16[8,128,96]{1,2,0:T(8,128)(2,1)}), bf16[8,128,96]{1,2,0:T(8,128)(2,1)S(1)}, u32[]{:S(2)}, u32[]{:S(2)}) %all-to-all-start.1) | async-done | bytes 196640 | tf_op jit(solution)/shard_map/all_to_all | solution.py:117
  36.3 3.4 %all-to-all-start.2 = ((bf16[8,128,96]{1,2,0:T(8,128)(2,1)}), bf16[8,128,96]{1,2,0:T(8,128)(2,1)S(1)}, u32[]{:S(2)}, u32[]{:S(2)}) async-start(bf16[8,128,96]{1,2,0:T(8,128)(2,1)} %bitcast.7), calls=%async_computation.2 | async-start | bytes 393216 | tf_op jit(solution)/shard_map/all_to_all | solution.py:118
  40.0 7.3 %all-to-all-done.2 = bf16[8,128,96]{1,2,0:T(8,128)(2,1)S(1)} async-done(((bf16[8,128,96]{1,2,0:T(8,128)(2,1)}), bf16[8,128,96]{1,2,0:T(8,128)(2,1)S(1)}, u32[]{:S(2)}, u32[]{:S(2)}) %all-to-all-start.2) | async-done | bytes 196640 | tf_op jit(solution)/shard_map/all_to_all | solution.py:118
  47.6 4.6 %while.24 = (s32[]{:T(128)}, bf16[2,512,96]{1,2,0:T(8,128)(2,1)S(1)}, f32[2,512]{1,0:T(2,128)S(1)}, bf16[2,512,96]{2,1,0:T(8,128)(2,1)S(1)}, bf16[1024,96]{1,0:T...) while((s32[]{:T(128)}, ...), condition=%wide.region_3.4_spmd.clone, body=%wide.region_0.3_spmd.clone.sunk | while | flops 204997120 | bytes 7164021 | solution.py:45
  52.3 0.9 copy.102
  53.2 2.6 reshape.122
  56.3 3.7 %reduce.63 = bf16[1024,96]{1,0:T(8,128)(2,1)} reduce(bf16[1024,1,96]{2,1,0:T(2,128)(2,1)} %bitcast.115, bf16[]{:T(256)} %broadcast.73), dimensions={1}, to_apply=%bitcast.66.reduce_sub_computation | reduce | bytes 393218
  60.1 2.1 reshape.155
  62.1 3.4 %all-to-all-start.3 = ((bf16[8,2,6144]{2,1,0:T(2,128)(2,1)}), bf16[8,2,6144]{2,1,0:T(2,128)(2,1)S(1)}, u32[]{:S(2)}, u32[]{:S(2)}) async-start(bf16[8,2,6144]{2,1,0:T(2,128)(2,1)} %reshape.155), calls=%async_computation.3 | async-start | bytes 393216 | tf_op jit(solution)/shard_map/all_to_all | solution.py:125
  66.8 2.5 slice_reduce_fusion.30
  69.3 3.9 %all-to-all-done.3 = bf16[8,2,6144]{2,1,0:T(2,128)(2,1)S(1)} async-done(((bf16[8,2,6144]{2,1,0:T(2,128)(2,1)}), bf16[8,2,6144]{2,1,0:T(2,128)(2,1)S(1)}, u32[]{:S(2)}, u32[]{:S(2)}) %all-to-all-start.3) | async-done | bytes 196640 | tf_op jit(solution)/shard_map/all_to_all | solution.py:125
  73.2 1.1 reshape.156
  74.3 1.2 copy.87
  75.9 2.7 broadcast_select_fusion
  78.6 1.9 collective-permute-start
  80.6 1.3 collective-permute-start.1
  81.9 1.6 slice_reduce_fusion.29
  83.5 3.0 collective-permute-done.1
  86.9 7.5 %multiply_reduce_fusion = (f32[1536]{0:T(1024)}, f32[1536]{0:T(1024)}, f32[1536]{0:T(1024)}, f32[1536]{0:T(1024)}, f32[1536]{0:T(1024)}, /*index=5*/f32[1536]{0:...) fusion(f32[158,1536]{1,0:T(8,128)S(1)} %maximum_convert_fusion,, ...), kind=kLoop, calls=%fused_computation.190 | loop fusion | flops 21206016 | bytes 26652800 | tf_op jit(solution)/shard_map/reduce_sum | solution.py:143
  94.4 1.3 collective-permute-start.2
  95.7 5.0 %collective-permute-start.3 = (f32[15,1536]{1,0:T(8,128)S(1)}, f32[15,1536]{1,0:T(8,128)S(1)}, u32[]{:S(2)}, u32[]{:S(2)}) collective-permute-start(f32[15,1536]{1,0:T(8,128)S(1)} %get-tuple-element.306), channel_id=1, source_target_pairs={{0,4},{4,8},{8,12},{12,16},{16,20},{20,24},{24,28},{1,5},{5,9},{9,... | collective-permute-start | bytes 276488 | tf_op jit(solution)/shard_map/ppermute | solution.py:21
  101.2 1.5 collective-permute-done.3
  102.7 3.7 %fusion.37 = bf16[128,1536]{1,0:T(8,128)(2,1)S(1)} fusion(f32[128,1536]{1,0:T(8,128)S(1)} %get-tuple-element.299, f32[15,1536]{1,0:T(8,128)S(1)} %collective-permute-done.3, f32[15,1536]{1,0:T(8,128)S(1)} %collective-permute-done.2, bf16[1,128,1536]{2,1,0:T(8,128)(2,1)S(1)} %copy-done.11, f32[1536]{0:T(1024)S(1)} %get-tuple-element.265, ...), kind=kLoop, calls=%fused_computation.100 | loop fusion | flops 18874368 | bytes 1947776 | tf_op jit(solution)/shard_map/convert_element_type | solution.py:151
  106.5 0.7 copy-done.8
  107.2 2.9 fusion.130
  110.2 0.9 copy.91
  111.1 2.1 reshape.121
  113.2 1.5 convolution_convert_fusion
  114.7 0.8 copy.89
  115.5 6.7 %all-to-all-start.4 = ((bf16[8,128,96]{1,2,0:T(8,128)(2,1)}), bf16[8,128,96]{1,2,0:T(8,128)(2,1)S(1)}, u32[]{:S(2)}, u32[]{:S(2)}) async-start(bf16[8,128,96]{1,2,0:T(8,128)(2,1)} %bitcast.121), calls=%async_computation.4 | async-start | bytes 393216 | tf_op jit(solution)/shard_map/all_to_all | solution.py:157
  122.4 3.0 multiply_reduce_fusion.18
  128.9 3.5 %stack.127 = f32[31,1536]{1,0:T(8,128)} concatenate(f32[1,1536]{1,0:T(1,128)} %stack.96, f32[1,1536]{1,0:T(1,128)} %stack.97, f32[1,1536]{1,0:T(1,128)} %stack.98, f32[1,1536]{1,0:T(1,128)} %stack.99, f32[1,1536]{1,0:T(1,128)} %stack.100, f32[1,1536]{1,0:T(1,128)S(1)} %stack.101, f32[1,1536]{1,0:T(1,128)S(1)} %stack.102, f32[1,1536]{1,0:T(1,128)S(1)} %stack.103, ...), dimensions={0} | concatenate | bytes 380928 | tf_op jit(solution)/shard_map/stack | solution.py:142
  132.4 1.5 all-to-all-done.4
  133.9 1.1 fusion.124
  135.0 0.8 copy.103
  135.8 0.7 broadcast.26
  136.5 12.9 %while.25 = (s32[]{:T(128)}, bf16[2,512,96]{1,2,0:T(8,128)(2,1)}, bf16[2,512,96]{2,1,0:T(8,128)(2,1)S(1)}, bf16[1024,96]{1,0:T(8,128)(2,1)S(1)}, f32[2,512]{1,0:...) while((s32[]{:T(128)}, bf16[2,512,96]{1,2,0:T(8,128)(2,1)}, ...), condition=%wide.region_6.7_spmd.clone, body=%wide.region_5.6_spmd.clone.sunk | while | flops 305185792 | bytes 6241429 | solution.py:73
  136.6 0.7 iota_compare_fusion.5
  138.0 1.8 fusion.162
  139.8 3.3 %fusion.163 = bf16[2,512,96]{1,2,0:T(8,128)(2,1)} fusion(bf16[2,512,96]{1,2,0:T(8,128)(2,1)} %get-tuple-element.455, s32[]{:T(128)S(6)} %copy.133, bf16[1024,96]{1,0:T(8,128)(2,1)S(1)} %get-tuple-element.467, f32[512,1024]{1,0:T(8,128)} %fusion.162, bf16[1024,96]{1,0:T(8,128)(2,1)S(1)} %get-tuple-element.470, f32[512]{0:T(512)S(1)} %bitcast.129, ...), kind=kOutput, calls=%fused_computation.17.clone.1 | convolution fusion | flops 204521472 | bytes 2955264 | tf_op jit(solution)/shard_map/while/body/eval_jaxpr/dot_general | solution.py:71
  143.0 0.7 iota_compare_fusion.5
  144.4 1.8 fusion.162
  146.2 3.2 fusion.163
  149.5 1.9 copy.104
  151.3 2.7 reshape.123
  154.0 3.7 %reduce.64 = bf16[1024,96]{1,0:T(8,128)(2,1)} reduce(bf16[1024,1,96]{2,1,0:T(2,128)(2,1)} %bitcast.116, bf16[]{:T(256)} %broadcast.73), dimensions={1}, to_apply=%bitcast.68.reduce_sub_computation | reduce | bytes 393218
  157.7 2.1 reshape.157
  159.8 4.5 %all-to-all-start.5 = ((bf16[8,2,6144]{2,1,0:T(2,128)(2,1)}), bf16[8,2,6144]{2,1,0:T(2,128)(2,1)}, u32[]{:S(2)}, u32[]{:S(2)}) async-start(bf16[8,2,6144]{2,1,0:T(2,128)(2,1)} %reshape.157), calls=%async_computation.5 | async-start | bytes 393216 | tf_op jit(solution)/shard_map/all_to_all | solution.py:165
  164.3 48.2 %reduce-scatter.2.cloned.1.call-done = f32[192,768]{1,0:T(8,128)} async-done(((f32[1536,768]{1,0:T(8,128)}), f32[192,768]{1,0:T(8,128)}) %reduce-scatter.2.cloned.1.call-update) | async-done | bytes 589840 | tf_op jit(solution)/shard_map/reduce_scatter | solution.py:170
  212.5 1.8 convert_element_type.98
  214.4 1.0 fusion.125
  215.4 40.3 %psum.23 = f32[1536]{0:T(1024)S(1)} all-reduce(f32[1536]{0:T(1024)S(1)} %copy-done.48), channel_id=1, replica_groups=mesh['seq'=8,'dp'=4] {'seq','dp'}, use_global_device_ids=true, to_apply=%region_42.43 | all-reduce | flops 1536 | bytes 12288 | tf_op jit(solution)/shard_map/psum | solution.py:172
  256.4 20.2 %all-reduce.5.cloned.1.call-done = f32[31,1536]{1,0:T(8,128)} async-done(((f32[31,1536]{1,0:T(8,128)}), f32[31,1536]{1,0:T(8,128)}) %all-reduce.5.cloned.1.call-update) | async-done | bytes 190480 | tf_op jit(solution)/shard_map/psum | solution.py:172
  276.6 1.5 constant_dynamic-slice_fusion.2
  278.0 1.3 reshape.158
  279.7 0.8 copy.101
  280.6 31.7 %all-reduce.3.cloned.1.call-done = bf16[192,768]{1,0:T(8,128)(2,1)} async-done(((bf16[192,768]{1,0:T(8,128)(2,1)}), bf16[192,768]{1,0:T(8,128)(2,1)}) %all-reduce.3.cloned.1.call-update) | async-done | bytes 294928 | tf_op jit(solution)/shard_map/psum | solution.py:171
  312.3 1.8 convert_element_type.99
  (178 shorter events, 12.9 us)
Async XLA Ops:
  8.0 67.7 %copy-start = (bf16[1536,768]{1,0:T(8,128)(2,1)S(1)}, bf16[1536,768]{1,0:T(8,128)(2,1)}, u32[]{:S(2)}) copy-start(bf16[1536,768]{1,0:T(8,128)(2,1)} %param.18) | copy-start | bytes 7077892
  9.9 15.2 %all-to-all-start = ((bf16[8,128,96]{1,2,0:T(8,128)(2,1)}), bf16[8,128,96]{1,2,0:T(8,128)(2,1)S(1)}, u32[]{:S(2)}, u32[]{:S(2)}) async-start(bf16[8,128,96]{1,2,0:T(8,128)(2,1)} %bitcast.3), calls=%async_computation | async-start | bytes 393216 | tf_op jit(solution)/shard_map/all_to_all | solution.py:107
  25.1 11.1 %all-to-all-start.1 = ((bf16[8,128,96]{1,2,0:T(8,128)(2,1)}), bf16[8,128,96]{1,2,0:T(8,128)(2,1)S(1)}, u32[]{:S(2)}, u32[]{:S(2)}) async-start(bf16[8,128,96]{1,2,0:T(8,128)(2,1)} %bitcast.5), calls=%async_computation.1 | async-start | bytes 393216 | tf_op jit(solution)/shard_map/all_to_all | solution.py:117
  36.3 11.1 %all-to-all-start.2 = ((bf16[8,128,96]{1,2,0:T(8,128)(2,1)}), bf16[8,128,96]{1,2,0:T(8,128)(2,1)S(1)}, u32[]{:S(2)}, u32[]{:S(2)}) async-start(bf16[8,128,96]{1,2,0:T(8,128)(2,1)} %bitcast.7), calls=%async_computation.2 | async-start | bytes 393216 | tf_op jit(solution)/shard_map/all_to_all | solution.py:118
  52.2 14.0 %copy-start.49 = (f32[2,512]{1,0:T(2,128)}, f32[2,512]{1,0:T(2,128)S(1)}, u32[]{:S(2)}) copy-start(f32[2,512]{1,0:T(2,128)S(1)} %get-tuple-element.448) | copy-start | bytes 12292
  52.3 23.3 %copy-start.1 = (bf16[1024,96]{1,0:T(8,128)(2,1)}, bf16[1024,96]{1,0:T(8,128)(2,1)S(1)}, u32[]{:S(2)}) copy-start(bf16[1024,96]{1,0:T(8,128)(2,1)S(1)} %get-tuple-element.477) | copy-start | bytes 589828
  52.3 23.3 %copy-start.3 = (bf16[1024,96]{1,0:T(8,128)(2,1)}, bf16[1024,96]{1,0:T(8,128)(2,1)S(1)}, u32[]{:S(2)}) copy-start(bf16[1024,96]{1,0:T(8,128)(2,1)S(1)} %get-tuple-element.480) | copy-start | bytes 589828
  52.3 23.3 %copy-start.5 = (bf16[2,512,96]{2,1,0:T(8,128)(2,1)}, bf16[2,512,96]{2,1,0:T(8,128)(2,1)S(1)}, u32[]{:S(2)}) copy-start(bf16[2,512,96]{2,1,0:T(8,128)(2,1)S(1)} %get-tuple-element.481) | copy-start | bytes 589828
  62.1 11.1 %all-to-all-start.3 = ((bf16[8,2,6144]{2,1,0:T(2,128)(2,1)}), bf16[8,2,6144]{2,1,0:T(2,128)(2,1)S(1)}, u32[]{:S(2)}, u32[]{:S(2)}) async-start(bf16[8,2,6144]{2,1,0:T(2,128)(2,1)} %reshape.155), calls=%async_computation.3 | async-start | bytes 393216 | tf_op jit(solution)/shard_map/all_to_all | solution.py:125
  65.5 147.0 %reduce-scatter.2.cloned.1.call-start = ((), (), s32[]{:S(2)}) async-start(), calls=%async_computation.7 | async-start | bytes 5308416 | tf_op jit(solution)/shard_map/reduce_scatter | solution.py:170
  75.7 11.0 %copy-start.11 = (bf16[1,128,1536]{2,1,0:T(8,128)(2,1)S(1)}, bf16[1,128,1536]{2,1,0:T(8,128)(2,1)}, u32[]{:S(2)}) copy-start(bf16[1,128,1536]{2,1,0:T(8,128)(2,1)} %param.21) | copy-start | bytes 1179652
  75.7 11.0 %copy-start.13 = (f32[1536]{0:T(1024)S(1)}, f32[1536]{0:T(1024)}, u32[]{:S(2)}) copy-start(f32[1536]{0:T(1024)} %get-tuple-element.238) | copy-start | bytes 18436
  75.7 11.0 %copy-start.14 = (f32[1536]{0:T(1024)S(1)}, f32[1536]{0:T(1024)}, u32[]{:S(2)}) copy-start(f32[1536]{0:T(1024)} %get-tuple-element.239) | copy-start | bytes 18436
  75.7 11.0 %copy-start.15 = (f32[1536]{0:T(1024)S(1)}, f32[1536]{0:T(1024)}, u32[]{:S(2)}) copy-start(f32[1536]{0:T(1024)} %get-tuple-element.240) | copy-start | bytes 18436
  75.7 11.0 %copy-start.16 = (f32[1536]{0:T(1024)S(1)}, f32[1536]{0:T(1024)}, u32[]{:S(2)}) copy-start(f32[1536]{0:T(1024)} %get-tuple-element.241) | copy-start | bytes 18436
  75.7 11.0 %copy-start.17 = (f32[1536]{0:T(1024)S(1)}, f32[1536]{0:T(1024)}, u32[]{:S(2)}) copy-start(f32[1536]{0:T(1024)} %get-tuple-element.242) | copy-start | bytes 18436
  75.7 11.0 %copy-start.18 = (f32[1536]{0:T(1024)S(1)}, f32[1536]{0:T(1024)}, u32[]{:S(2)}) copy-start(f32[1536]{0:T(1024)} %get-tuple-element.243) | copy-start | bytes 18436
  75.7 11.0 %copy-start.19 = (f32[1536]{0:T(1024)S(1)}, f32[1536]{0:T(1024)}, u32[]{:S(2)}) copy-start(f32[1536]{0:T(1024)} %get-tuple-element.244) | copy-start | bytes 18436
  75.7 11.0 %copy-start.20 = (f32[1536]{0:T(1024)S(1)}, f32[1536]{0:T(1024)}, u32[]{:S(2)}) copy-start(f32[1536]{0:T(1024)} %get-tuple-element.245) | copy-start | bytes 18436
  75.8 11.0 %copy-start.21 = (f32[1536]{0:T(1024)S(1)}, f32[1536]{0:T(1024)}, u32[]{:S(2)}) copy-start(f32[1536]{0:T(1024)} %get-tuple-element.246) | copy-start | bytes 18436
  75.8 11.0 %copy-start.22 = (f32[1536]{0:T(1024)S(1)}, f32[1536]{0:T(1024)}, u32[]{:S(2)}) copy-start(f32[1536]{0:T(1024)} %get-tuple-element.247) | copy-start | bytes 18436
  75.8 11.0 %copy-start.23 = (f32[1536]{0:T(1024)S(1)}, f32[1536]{0:T(1024)}, u32[]{:S(2)}) copy-start(f32[1536]{0:T(1024)} %get-tuple-element.248) | copy-start | bytes 18436
  75.8 11.0 %copy-start.24 = (f32[1536]{0:T(1024)S(1)}, f32[1536]{0:T(1024)}, u32[]{:S(2)}) copy-start(f32[1536]{0:T(1024)} %get-tuple-element.249) | copy-start | bytes 18436
  75.8 11.0 %copy-start.25 = (f32[1536]{0:T(1024)S(1)}, f32[1536]{0:T(1024)}, u32[]{:S(2)}) copy-start(f32[1536]{0:T(1024)} %get-tuple-element.250) | copy-start | bytes 18436
  75.8 11.0 %copy-start.26 = (f32[1536]{0:T(1024)S(1)}, f32[1536]{0:T(1024)}, u32[]{:S(2)}) copy-start(f32[1536]{0:T(1024)} %get-tuple-element.251) | copy-start | bytes 18436
  75.8 11.0 %copy-start.27 = (f32[1536]{0:T(1024)S(1)}, f32[1536]{0:T(1024)}, u32[]{:S(2)}) copy-start(f32[1536]{0:T(1024)} %get-tuple-element.252) | copy-start | bytes 18436
  75.8 11.0 %copy-start.28 = (f32[1536]{0:T(1024)S(1)}, f32[1536]{0:T(1024)}, u32[]{:S(2)}) copy-start(f32[1536]{0:T(1024)} %get-tuple-element.253) | copy-start | bytes 18436
  75.8 11.0 %copy-start.29 = (f32[1536]{0:T(1024)S(1)}, f32[1536]{0:T(1024)}, u32[]{:S(2)}) copy-start(f32[1536]{0:T(1024)} %get-tuple-element.254) | copy-start | bytes 18436
  75.8 11.0 %copy-start.50 = (pred[128]{0:T(512)(128)(4,1)S(1)}, pred[128]{0:T(512)(128)(4,1)}, u32[]{:S(2)}) copy-start(pred[128]{0:T(512)(128)(4,1)} %add_compare_fusion) | copy-start | bytes 388
  75.9 11.0 %copy-start.52 = (f32[1536]{0:T(1024)S(1)}, f32[1536]{0:T(1024)}, u32[]{:S(2)}) copy-start(f32[1536]{0:T(1024)} %param.20) | copy-start | bytes 18436
  78.6 4.9 %collective-permute-start = (bf16[15,1536]{1,0:T(8,128)(2,1)S(1)}, bf16[15,1536]{1,0:T(8,128)(2,1)S(1)}, u32[]{:S(2)}, u32[]{:S(2)}) collective-permute-start(bf16[15,1536]{1,0:T(8,128)(2,1)S(1)} %get-tuple-element.307), channel_id=1, source_target_pairs={{0,4},{4,8},{8,12},{12,16},{16,20},{20,24},{24,28},{1,5},{5,9},{9,... | collective-permute-start | bytes 138248 | tf_op jit(solution)/shard_map/ppermute | solution.py:21
  80.6 6.0 %collective-permute-start.1 = (bf16[15,1536]{1,0:T(8,128)(2,1)S(1)}, bf16[15,1536]{1,0:T(8,128)(2,1)S(1)}, u32[]{:S(2)}, u32[]{:S(2)}) collective-permute-start(bf16[15,1536]{1,0:T(8,128)(2,1)S(1)} %get-tuple-element.308), channel_id=1, source_target_pairs={{4,0},{8,4},{12,8},{16,12},{20,16},{24,20},{28,24},{5,1},{9,5},{13... | collective-permute-start | bytes 138248 | tf_op jit(solution)/shard_map/ppermute | solution.py:22
  94.4 8.3 %copy-start.7 = (f32[128,1536]{1,0:T(8,128)}, f32[128,1536]{1,0:T(8,128)S(1)}, u32[]{:S(2)}) copy-start(f32[128,1536]{1,0:T(8,128)S(1)} %get-tuple-element.299) | copy-start | bytes 2359300
  94.4 6.7 %collective-permute-start.2 = (f32[15,1536]{1,0:T(8,128)S(1)}, f32[15,1536]{1,0:T(8,128)S(1)}, u32[]{:S(2)}, u32[]{:S(2)}) collective-permute-start(f32[15,1536]{1,0:T(8,128)S(1)} %get-tuple-element.305), channel_id=1, source_target_pairs={{4,0},{8,4},{12,8},{16,12},{20,16},{24,20},{28,24},{5,1},{9,5},{13... | collective-permute-start | bytes 276488 | tf_op jit(solution)/shard_map/ppermute | solution.py:22
  95.7 7.0 %collective-permute-start.3 = (f32[15,1536]{1,0:T(8,128)S(1)}, f32[15,1536]{1,0:T(8,128)S(1)}, u32[]{:S(2)}, u32[]{:S(2)}) collective-permute-start(f32[15,1536]{1,0:T(8,128)S(1)} %get-tuple-element.306), channel_id=1, source_target_pairs={{0,4},{4,8},{8,12},{12,16},{16,20},{20,24},{24,28},{1,5},{5,9},{9,... | collective-permute-start | bytes 276488 | tf_op jit(solution)/shard_map/ppermute | solution.py:21
  115.5 18.4 %all-to-all-start.4 = ((bf16[8,128,96]{1,2,0:T(8,128)(2,1)}), bf16[8,128,96]{1,2,0:T(8,128)(2,1)S(1)}, u32[]{:S(2)}, u32[]{:S(2)}) async-start(bf16[8,128,96]{1,2,0:T(8,128)(2,1)} %bitcast.121), calls=%async_computation.4 | async-start | bytes 393216 | tf_op jit(solution)/shard_map/all_to_all | solution.py:157
  122.1 3.6 %copy-start.31 = (f32[1536]{0:T(1024)S(1)}, f32[1536]{0:T(1024)}, u32[]{:S(2)}) copy-start(f32[1536]{0:T(1024)} %get-tuple-element.220) | copy-start | bytes 18436
  122.1 3.7 %copy-start.30 = (f32[1536]{0:T(1024)S(1)}, f32[1536]{0:T(1024)}, u32[]{:S(2)}) copy-start(f32[1536]{0:T(1024)} %get-tuple-element.221) | copy-start | bytes 18436
  122.2 154.4 %all-reduce.5.cloned.1.call-start = ((), (), s32[]{:S(2)}) async-start(), calls=%async_computation.9 | async-start | bytes 393216 | tf_op jit(solution)/shard_map/psum | solution.py:172
  122.2 3.2 copy-start.46
  122.2 3.2 %copy-start.45 = (f32[1536]{0:T(1024)S(1)}, f32[1536]{0:T(1024)}, u32[]{:S(2)}) copy-start(f32[1536]{0:T(1024)} %get-tuple-element.206) | copy-start | bytes 18436
  122.2 3.2 %copy-start.44 = (f32[1536]{0:T(1024)S(1)}, f32[1536]{0:T(1024)}, u32[]{:S(2)}) copy-start(f32[1536]{0:T(1024)} %get-tuple-element.207) | copy-start | bytes 18436
  122.3 3.2 %copy-start.43 = (f32[1536]{0:T(1024)S(1)}, f32[1536]{0:T(1024)}, u32[]{:S(2)}) copy-start(f32[1536]{0:T(1024)} %get-tuple-element.208) | copy-start | bytes 18436
  122.3 3.3 %copy-start.42 = (f32[1536]{0:T(1024)S(1)}, f32[1536]{0:T(1024)}, u32[]{:S(2)}) copy-start(f32[1536]{0:T(1024)} %get-tuple-element.209) | copy-start | bytes 18436
  122.3 3.3 %copy-start.41 = (f32[1536]{0:T(1024)S(1)}, f32[1536]{0:T(1024)}, u32[]{:S(2)}) copy-start(f32[1536]{0:T(1024)} %get-tuple-element.210) | copy-start | bytes 18436
  122.3 3.3 %copy-start.40 = (f32[1536]{0:T(1024)S(1)}, f32[1536]{0:T(1024)}, u32[]{:S(2)}) copy-start(f32[1536]{0:T(1024)} %get-tuple-element.211) | copy-start | bytes 18436
  122.3 3.3 %copy-start.39 = (f32[1536]{0:T(1024)S(1)}, f32[1536]{0:T(1024)}, u32[]{:S(2)}) copy-start(f32[1536]{0:T(1024)} %get-tuple-element.212) | copy-start | bytes 18436
  122.3 3.3 %copy-start.38 = (f32[1536]{0:T(1024)S(1)}, f32[1536]{0:T(1024)}, u32[]{:S(2)}) copy-start(f32[1536]{0:T(1024)} %get-tuple-element.213) | copy-start | bytes 18436
  122.3 3.3 %copy-start.37 = (f32[1536]{0:T(1024)S(1)}, f32[1536]{0:T(1024)}, u32[]{:S(2)}) copy-start(f32[1536]{0:T(1024)} %get-tuple-element.214) | copy-start | bytes 18436
  122.3 3.3 %copy-start.36 = (f32[1536]{0:T(1024)S(1)}, f32[1536]{0:T(1024)}, u32[]{:S(2)}) copy-start(f32[1536]{0:T(1024)} %get-tuple-element.215) | copy-start | bytes 18436
  122.3 3.4 %copy-start.35 = (f32[1536]{0:T(1024)S(1)}, f32[1536]{0:T(1024)}, u32[]{:S(2)}) copy-start(f32[1536]{0:T(1024)} %get-tuple-element.216) | copy-start | bytes 18436
  122.3 3.4 %copy-start.34 = (f32[1536]{0:T(1024)S(1)}, f32[1536]{0:T(1024)}, u32[]{:S(2)}) copy-start(f32[1536]{0:T(1024)} %get-tuple-element.217) | copy-start | bytes 18436
  122.4 3.4 %copy-start.33 = (f32[1536]{0:T(1024)S(1)}, f32[1536]{0:T(1024)}, u32[]{:S(2)}) copy-start(f32[1536]{0:T(1024)} %get-tuple-element.218) | copy-start | bytes 18436
  122.4 3.4 %copy-start.32 = (f32[1536]{0:T(1024)S(1)}, f32[1536]{0:T(1024)}, u32[]{:S(2)}) copy-start(f32[1536]{0:T(1024)} %get-tuple-element.219) | copy-start | bytes 18436
  125.4 11.2 %copy-start.2 = (bf16[1024,96]{1,0:T(8,128)(2,1)S(1)}, bf16[1024,96]{1,0:T(8,128)(2,1)}, u32[]{:S(2)}) copy-start(bf16[1024,96]{1,0:T(8,128)(2,1)} %copy-done.1) | copy-start | bytes 589828
  125.4 11.2 %copy-start.4 = (bf16[1024,96]{1,0:T(8,128)(2,1)S(1)}, bf16[1024,96]{1,0:T(8,128)(2,1)}, u32[]{:S(2)}) copy-start(bf16[1024,96]{1,0:T(8,128)(2,1)} %copy-done.3) | copy-start | bytes 589828
  125.4 11.2 %copy-start.6 = (bf16[2,512,96]{2,1,0:T(8,128)(2,1)S(1)}, bf16[2,512,96]{2,1,0:T(8,128)(2,1)}, u32[]{:S(2)}) copy-start(bf16[2,512,96]{2,1,0:T(8,128)(2,1)} %copy-done.5) | copy-start | bytes 589828
  136.6 3.2 copy-start.12
  149.4 64.9 %copy-start.9 = (f32[128,1536]{1,0:T(8,128)S(1)}, f32[128,1536]{1,0:T(8,128)}, u32[]{:S(2)}) copy-start(f32[128,1536]{1,0:T(8,128)} %get-tuple-element.300) | copy-start | bytes 2359300
  149.5 64.9 %copy-start.10 = (bf16[128,1536]{1,0:T(8,128)(2,1)S(1)}, bf16[128,1536]{1,0:T(8,128)(2,1)}, u32[]{:S(2)}) copy-start(bf16[128,1536]{1,0:T(8,128)(2,1)} %get-tuple-element.310) | copy-start | bytes 1179652
  149.5 64.9 %copy-start.51 = (pred[128]{0:T(512)(128)(4,1)S(1)}, pred[128]{0:T(512)(128)(4,1)}, u32[]{:S(2)}) copy-start(pred[128]{0:T(512)(128)(4,1)} %add_compare_fusion) | copy-start | bytes 388
  154.0 61.4 %copy-start.48 = (f32[1536]{0:T(1024)S(1)}, f32[1536]{0:T(1024)}, u32[]{:S(2)}) copy-start(f32[1536]{0:T(1024)} %get-tuple-element.235) | copy-start | bytes 18436
  159.8 118.3 %all-to-all-start.5 = ((bf16[8,2,6144]{2,1,0:T(2,128)(2,1)}), bf16[8,2,6144]{2,1,0:T(2,128)(2,1)}, u32[]{:S(2)}, u32[]{:S(2)}) async-start(bf16[8,2,6144]{2,1,0:T(2,128)(2,1)} %reshape.157), calls=%async_computation.5 | async-start | bytes 393216 | tf_op jit(solution)/shard_map/all_to_all | solution.py:165
  164.2 148.0 %all-reduce.3.cloned.1.call-start = ((), (), s32[]{:S(2)}) async-start(), calls=%async_computation.8 | async-start | bytes 589824 | tf_op jit(solution)/shard_map/psum | solution.py:171
  (3 other events, 7.1 us)
Sparse Core Ops, SparseCore 0:
  110.3 102.1 reduce-scatter.1
Sparse Core Ops, SparseCore 1:
  132.5 144.0 all-reduce.4
  279.3 32.9 all-reduce.2
where the time goes:
time: 324 us; the launch traced here: 322 us
  waiting for transfers between devices  130 us (40%)
  local copies, waits for them, and re-layouts  44.2 us (14%)
  blocking collectives  40.3 us (12%)
  starting transfers between devices  38.2 us (12%)
  other arithmetic  31.9 us (10%)
  matrix products  19.4 us (6%)
  between operations  17.3 us (5%)
    reduce_scatter x1, waiting for transfers between devices, on_device(): lax.psum_scatter(term_block, 'seq', scatter_dimension=0, tiled=True)  48.2 us
    psum x1, blocking collectives, on_device(): lax.psum((kernel_local, bias_local), ('seq', 'dp'))  40.3 us
    psum x1, waiting for transfers between devices, on_device(): lax.psum(partial_rows.astype(jnp.bfloat16), 'dp').astype(jnp.float32)  31.7 us
    psum x1, waiting for transfers between devices, on_device(): lax.psum((kernel_local, bias_local), ('seq', 'dp'))  20.2 us
    unnamed x119, local copies, waits for them, and re-layouts  15.6 us
    reduce_sum x2, other arithmetic, on_device(): jnp.sum(grad_conv * padded[tap:tap + frames_dev], axis=0)  10.5 us
    unnamed x2, other arithmetic  7.45 us
    all_to_all x1, waiting for transfers between devices, on_device(): lax.all_to_all(value_send, 'seq', split_axis=0, concat_axis=1, tiled=True)  7.34 us
  transfers between devices with their start and end apart: 13, of which 11 were waited for; matrix products, arithmetic and copies ran while one was open for 18% of the time, Pallas kernels for 0%

commit v1 on v0

--- a/solution.py
+++ b/solution.py
@@ -169,7 +169,7 @@
     )
     partial_rows = lax.psum_scatter(term_block, "seq", scatter_dimension=0, tiled=True)
     summed = lax.psum(partial_rows.astype(jnp.bfloat16), "dp").astype(jnp.float32)
-    kernel_total, bias_total = lax.psum((kernel_local, bias_local), ("seq", "dp"))
+    kernel_total, bias_total = lax.psum(lax.psum((kernel_local, bias_local), "dp"), "seq")
     shard_width = D // seq_count
     offset = lax.axis_index("seq") * shard_width
     grad_kernel = lax.dynamic_slice_in_dim(kernel_total, offset, shard_width, 1)

time: 324 us -> 361 us (1.11)
  waiting for transfers between devices: 130 us -> 160 us
  blocking collectives: 40.3 us -> 27.3 us
  other arithmetic: 31.9 us -> 43.5 us
  local copies, waits for them, and re-layouts: 44.2 us -> 54.4 us
    psum x1 -> x2, waiting for transfers between devices: 20.2 us -> 42.1 us  [the longest x1 42.1 us: on_device(): lax.psum(lax.psum((kernel_local, bias_local), 'dp'), 'seq')]
    convert_element_type x1, other arithmetic: 3.73 us -> 17.2 us  [on_device(): (grad_rows + jnp.where(local_valid[:, None], grad_masked, 0.0)).astype(jn...]
    psum x1 -> x2, blocking collectives: 40.3 us -> 27.3 us  [the longest x1 20.9 us: on_device(): lax.psum(lax.psum((kernel_local, bias_local), 'dp'), 'seq')]
    another operation x32, local copies, waits for them, and re-layouts: 6.65 us -> 16.5 us  [on_device(): jnp.stack([jnp.sum(grad_conv * padded[tap:tap + frames_dev], axis=0) for...]
    reduce_scatter x1, waiting for transfers between devices: 48.2 us -> 54.5 us  [on_device(): lax.psum_scatter(term_block, 'seq', scatter_dimension=0, tiled=True)]
    all_to_all x1, waiting for transfers between devices: 1.46 us -> 7.2 us  [on_device(): lax.all_to_all(to_serving(grad_attn), 'seq', split_axis=0, concat_axis=1,...]
    unnamed x119 -> x103, local copies, waits for them, and re-layouts: 15.6 us -> 15.5 us
  transfers between devices with their start and end apart: 13 -> 14, of which waited for: 11 -> 9; matrix products, arithmetic and copies ran while one was open for 18% -> 24% of each run, Pallas kernels for 0% -> 0%
where the time goes in v1:
time: 361 us; the launch traced here: 359 us
  waiting for transfers between devices  160 us (44%)
  local copies, waits for them, and re-layouts  54.4 us (15%)
  other arithmetic  43.5 us (12%)
  starting transfers between devices  36 us (10%)
  blocking collectives  27.3 us (8%)
  matrix products  20.2 us (6%)
  between operations  17.2 us (5%)
    reduce_scatter x1, waiting for transfers between devices, on_device(): lax.psum_scatter(term_block, 'seq', scatter_dimension=0, tiled=True)  54.5 us
    psum x1, waiting for transfers between devices, on_device(): lax.psum(lax.psum((kernel_local, bias_local), 'dp'), 'seq')  42.1 us
    psum x1, waiting for transfers between devices, on_device(): lax.psum(partial_rows.astype(jnp.bfloat16), 'dp').astype(jnp.float32)  29.9 us
    psum x1, blocking collectives, on_device(): lax.psum(lax.psum((kernel_local, bias_local), 'dp'), 'seq')  20.9 us
    convert_element_type x1, other arithmetic, on_device(): (grad_rows + jnp.where(local_valid[:, None], grad_masked, 0.0)).astype(jn...  17.2 us
    another operation x32, local copies, waits for them, and re-layouts, on_device(): jnp.stack([jnp.sum(grad_conv * padded[tap:tap + frames_dev], axis=0) for...  16.5 us
    unnamed x103, local copies, waits for them, and re-layouts  15.5 us
    reduce_sum x2, other arithmetic, on_device(): jnp.sum(grad_conv * padded[tap:tap + frames_dev], axis=0)  8.57 us
  transfers between devices with their start and end apart: 14, of which 9 were waited for; matrix products, arithmetic and copies ran while one was open for 24% of the time, Pallas kernels for 0%

profile of v1, /device:TPU:0, one launch (start us, length us, event | category | flops | bytes accessed | tf_op | source)
XLA Modules:
  0.0 358.9 jit_solution(13610677244165978898)
XLA Ops:
  8.0 1.9 copy.76
  9.9 7.3 %all-to-all-start = ((bf16[8,128,96]{1,2,0:T(8,128)(2,1)}), bf16[8,128,96]{1,2,0:T(8,128)(2,1)S(1)}, u32[]{:S(2)}, u32[]{:S(2)}) async-start(bf16[8,128,96]{1,2,0:T(8,128)(2,1)} %bitcast.3), calls=%async_computation | async-start | bytes 393216 | tf_op jit(solution)/shard_map/all_to_all | solution.py:107
  17.2 1.7 copy.78
  18.9 6.2 %all-to-all-done = bf16[8,128,96]{1,2,0:T(8,128)(2,1)S(1)} async-done(((bf16[8,128,96]{1,2,0:T(8,128)(2,1)}), bf16[8,128,96]{1,2,0:T(8,128)(2,1)S(1)}, u32[]{:S(2)}, u32[]{:S(2)}) %all-to-all-start) | async-done | bytes 196640 | tf_op jit(solution)/shard_map/all_to_all | solution.py:107
  25.1 3.4 all-to-all-start.1
  28.5 1.7 copy.80
  30.3 6.0 %all-to-all-done.1 = bf16[8,128,96]{1,2,0:T(8,128)(2,1)S(1)} async-done(((bf16[8,128,96]{1,2,0:T(8,128)(2,1)}), bf16[8,128,96]{1,2,0:T(8,128)(2,1)S(1)}, u32[]{:S(2)}, u32[]{:S(2)}) %all-to-all-start.1) | async-done | bytes 196640 | tf_op jit(solution)/shard_map/all_to_all | solution.py:117
  36.3 3.4 all-to-all-start.2
  40.0 7.3 %all-to-all-done.2 = bf16[8,128,96]{1,2,0:T(8,128)(2,1)S(1)} async-done(((bf16[8,128,96]{1,2,0:T(8,128)(2,1)}), bf16[8,128,96]{1,2,0:T(8,128)(2,1)S(1)}, u32[]{:S(2)}, u32[]{:S(2)}) %all-to-all-start.2) | async-done | bytes 196640 | tf_op jit(solution)/shard_map/all_to_all | solution.py:118
  47.6 4.6 %while.24 = (s32[]{:T(128)}, bf16[2,512,96]{1,2,0:T(8,128)(2,1)S(1)}, f32[2,512]{1,0:T(2,128)S(1)}, bf16[2,512,96]{2,1,0:T(8,128)(2,1)S(1)}, bf16[1024,96]{1,0:T...) while((s32[]{:T(128)}, ...), condition=%wide.region_3.4_spmd.clone, body=%wide.region_0.3_spmd.clone.sunk | while | flops 204997120 | bytes 7164021 | solution.py:45
  47.6 0.7 iota_compare_fusion.4
  52.3 0.8 copy.102
  53.1 2.6 reshape.122
  56.3 3.8 %reduce.63 = bf16[1024,96]{1,0:T(8,128)(2,1)} reduce(bf16[1024,1,96]{2,1,0:T(2,128)(2,1)} %bitcast.115, bf16[]{:T(256)} %broadcast.73), dimensions={1}, to_apply=%bitcast.66.reduce_sub_computation | reduce | bytes 393218
  60.1 2.1 reshape.155
  62.1 3.4 all-to-all-start.3
  66.8 2.5 slice_reduce_fusion.30
  69.3 3.9 %all-to-all-done.3 = bf16[8,2,6144]{2,1,0:T(2,128)(2,1)S(1)} async-done(((bf16[8,2,6144]{2,1,0:T(2,128)(2,1)}), bf16[8,2,6144]{2,1,0:T(2,128)(2,1)S(1)}, u32[]{:S(2)}, u32[]{:S(2)}) %all-to-all-start.3) | async-done | bytes 196640 | tf_op jit(solution)/shard_map/all_to_all | solution.py:125
  73.3 1.1 reshape.156
  74.3 1.2 copy.87
  75.9 2.8 broadcast_select_fusion
  78.7 1.9 collective-permute-start
  80.7 1.3 collective-permute-start.1
  82.0 1.6 slice_reduce_fusion.29
  83.7 2.9 collective-permute-done.1
  87.0 6.8 %multiply_reduce_fusion = (f32[1536]{0:T(1024)S(1)}, f32[1536]{0:T(1024)S(1)}, f32[1536]{0:T(1024)S(1)}, f32[1536]{0:T(1024)S(1)}, f32[1536]{0:T(1024)S(1)}, /*i...) fusion(f32[158,1536]{1,0:T(8,128)S(1)} %maximum_convert_fusion,, ...), kind=kLoop, calls=%fused_computation.190 | loop fusion | flops 21206016 | bytes 26652800 | tf_op jit(solution)/shard_map/reduce_sum | solution.py:143
  93.9 1.3 collective-permute-start.2
  95.2 5.4 %collective-permute-start.3 = (f32[15,1536]{1,0:T(8,128)S(1)}, f32[15,1536]{1,0:T(8,128)}, u32[]{:S(2)}, u32[]{:S(2)}) collective-permute-start(f32[15,1536]{1,0:T(8,128)S(1)} %get-tuple-element.306), channel_id=1, source_target_pairs={{0,4},{4,8},{8,12},{12,16},{16,20},{20,24},{24,28},{1,5},{5,9},{9,... | collective-permute-start | bytes 276488 | tf_op jit(solution)/shard_map/ppermute | solution.py:21
  100.6 1.8 multiply_reduce_fusion.18
  113.9 5.1 %stack.127 = f32[31,1536]{1,0:T(8,128)} concatenate(f32[1,1536]{1,0:T(1,128)} %stack.96, f32[1,1536]{1,0:T(1,128)} %stack.97, f32[1,1536]{1,0:T(1,128)} %stack.98, f32[1,1536]{1,0:T(1,128)} %stack.99, f32[1,1536]{1,0:T(1,128)} %stack.100, f32[1,1536]{1,0:T(1,128)} %stack.101, f32[1,1536]{1,0:T(1,128)} %stack.102, f32[1,1536]{1,0:T(1,128)} %stack.103, f32[1,1536]{1,0:T(1,128)} %stack.104, ...), dimensions={0} | concatenate | bytes 380928 | tf_op jit(solution)/shard_map/stack | solution.py:142
  119.9 17.2 %fusion.37 = bf16[128,1536]{1,0:T(8,128)(2,1)S(1)} fusion(f32[128,1536]{1,0:T(8,128)} %copy-done.1, f32[15,1536]{1,0:T(8,128)} %collective-permute-done.3, f32[15,1536]{1,0:T(8,128)} %copy-done.9, bf16[1,128,1536]{2,1,0:T(8,128)(2,1)} %param.21, f32[1536]{0:T(1024)} %copy-done.37, f32[1536]{0:T(1024)} %copy-done.38, f32[1536]{0:T(1024)S(1)} %get-tuple-element.237, ...), kind=kLoop, calls=%fused_computation.100 | loop fusion | flops 18874368 | bytes 1947776 | tf_op jit(solution)/shard_map/convert_element_type | solution.py:151
  137.1 4.0 %fusion.130 = f32[1536,768]{1,0:T(8,128)} fusion(bf16[128,1536]{1,0:T(8,128)(2,1)S(1)} %fusion.37, bf16[128,768]{0,1:T(8,128)(2,1)} %bitcast.120), kind=kOutput, calls=%fused_computation.265 | convolution fusion | flops 301989888 | bytes 5308416 | tf_op jit(solution)/shard_map/dot_general | solution.py:167
  141.2 1.2 convolution_convert_fusion
  142.3 1.7 copy.89
  144.1 4.2 %all-to-all-start.4 = ((bf16[8,128,96]{1,2,0:T(8,128)(2,1)}), bf16[8,128,96]{1,2,0:T(8,128)(2,1)S(1)}, u32[]{:S(2)}, u32[]{:S(2)}) async-start(bf16[8,128,96]{1,2,0:T(8,128)(2,1)} %bitcast.14), calls=%async_computation.4 | async-start | bytes 393216 | tf_op jit(solution)/shard_map/all_to_all | solution.py:157
  148.3 1.9 copy.91
  150.2 2.1 reshape.121
  152.3 7.2 %all-to-all-done.4 = bf16[8,128,96]{1,2,0:T(8,128)(2,1)S(1)} async-done(((bf16[8,128,96]{1,2,0:T(8,128)(2,1)}), bf16[8,128,96]{1,2,0:T(8,128)(2,1)S(1)}, u32[]{:S(2)}, u32[]{:S(2)}) %all-to-all-start.4) | async-done | bytes 196640 | tf_op jit(solution)/shard_map/all_to_all | solution.py:157
  159.5 1.1 fusion.124
  160.6 0.8 copy.103
  161.4 0.7 broadcast.26
  162.1 11.5 %while.25 = (s32[]{:T(128)}, bf16[2,512,96]{1,2,0:T(8,128)(2,1)}, bf16[2,512,96]{2,1,0:T(8,128)(2,1)S(1)}, bf16[1024,96]{1,0:T(8,128)(2,1)S(1)}, f32[2,512]{1,0:...) while((s32[]{:T(128)}, bf16[2,512,96]{1,2,0:T(8,128)(2,1)}, ...), condition=%wide.region_6.7_spmd.clone, body=%wide.region_5.6_spmd.clone.sunk | while | flops 305185792 | bytes 6241429 | solution.py:73
  162.1 0.7 iota_compare_fusion.5
  162.9 1.8 fusion.162
  164.7 3.2 fusion.163
  167.9 0.7 iota_compare_fusion.5
  168.6 1.8 fusion.162
  170.4 3.2 fusion.163
  173.6 1.9 copy.104
  175.5 2.6 reshape.123
  178.2 3.8 %reduce.64 = bf16[1024,96]{1,0:T(8,128)(2,1)} reduce(bf16[1024,1,96]{2,1,0:T(2,128)(2,1)} %bitcast.116, bf16[]{:T(256)} %broadcast.73), dimensions={1}, to_apply=%bitcast.68.reduce_sub_computation | reduce | bytes 393218
  182.0 2.1 reshape.157
  184.0 4.0 %all-to-all-start.5 = ((bf16[8,2,6144]{2,1,0:T(2,128)(2,1)}), bf16[8,2,6144]{2,1,0:T(2,128)(2,1)}, u32[]{:S(2)}, u32[]{:S(2)}) async-start(bf16[8,2,6144]{2,1,0:T(2,128)(2,1)} %reshape.157), calls=%async_computation.5 | async-start | bytes 393216 | tf_op jit(solution)/shard_map/all_to_all | solution.py:165
  188.1 54.5 %reduce-scatter.2.cloned.1.call-done = f32[192,768]{1,0:T(8,128)} async-done(((f32[1536,768]{1,0:T(8,128)}), f32[192,768]{1,0:T(8,128)}) %reduce-scatter.2.cloned.1.call-update) | async-done | bytes 589840 | tf_op jit(solution)/shard_map/reduce_scatter | solution.py:170
  242.6 1.8 convert_element_type.98
  244.5 1.0 fusion.125
  245.5 6.4 %psum.38 = f32[1536]{0:T(1024)S(1)} all-reduce(f32[1536]{0:T(1024)S(1)} %copy-done.39), channel_id=1, replica_groups=mesh['seq'=8,'dp'=4] {'dp'}, use_global_device_ids=true, to_apply=%region_43.44 | all-reduce | flops 1536 | bytes 12288 | tf_op jit(solution)/shard_map/psum | solution.py:172
  251.9 20.9 %psum.39 = f32[1536]{0:T(1024)S(1)} all-reduce(f32[1536]{0:T(1024)S(1)} %psum.38), channel_id=1, replica_groups=mesh['seq'=8,'dp'=4] {'seq'}, use_global_device_ids=true, to_apply=%region_44.45 | all-reduce | flops 1536 | bytes 12288 | tf_op jit(solution)/shard_map/psum | solution.py:172
  273.5 42.1 %all-reduce.8.cloned.1.call-done = f32[31,1536]{1,0:T(8,128)} async-done(((f32[31,1536]{1,0:T(8,128)}), f32[31,1536]{1,0:T(8,128)}) %all-reduce.8.cloned.1.call-update) | async-done | bytes 190480 | tf_op jit(solution)/shard_map/psum | solution.py:172
  315.6 1.5 constant_dynamic-slice_fusion.2
  317.1 1.3 reshape.158
  318.8 0.8 copy.101
  319.6 29.9 %all-reduce.4.cloned.1.call-done = bf16[192,768]{1,0:T(8,128)(2,1)} async-done(((bf16[192,768]{1,0:T(8,128)(2,1)}), bf16[192,768]{1,0:T(8,128)(2,1)}) %all-reduce.4.cloned.1.call-update) | async-done | bytes 294928 | tf_op jit(solution)/shard_map/psum | solution.py:171
  349.5 1.8 convert_element_type.99
  (166 shorter events, 19.6 us)
Async XLA Ops:
  8.0 67.7 %copy-start = (bf16[1536,768]{1,0:T(8,128)(2,1)S(1)}, bf16[1536,768]{1,0:T(8,128)(2,1)}, u32[]{:S(2)}) copy-start(bf16[1536,768]{1,0:T(8,128)(2,1)} %param.18) | copy-start | bytes 7077892
  9.9 15.2 %all-to-all-start = ((bf16[8,128,96]{1,2,0:T(8,128)(2,1)}), bf16[8,128,96]{1,2,0:T(8,128)(2,1)S(1)}, u32[]{:S(2)}, u32[]{:S(2)}) async-start(bf16[8,128,96]{1,2,0:T(8,128)(2,1)} %bitcast.3), calls=%async_computation | async-start | bytes 393216 | tf_op jit(solution)/shard_map/all_to_all | solution.py:107
  25.1 11.1 %all-to-all-start.1 = ((bf16[8,128,96]{1,2,0:T(8,128)(2,1)}), bf16[8,128,96]{1,2,0:T(8,128)(2,1)S(1)}, u32[]{:S(2)}, u32[]{:S(2)}) async-start(bf16[8,128,96]{1,2,0:T(8,128)(2,1)} %bitcast.5), calls=%async_computation.1 | async-start | bytes 393216 | tf_op jit(solution)/shard_map/all_to_all | solution.py:117
  36.3 11.1 %all-to-all-start.2 = ((bf16[8,128,96]{1,2,0:T(8,128)(2,1)}), bf16[8,128,96]{1,2,0:T(8,128)(2,1)S(1)}, u32[]{:S(2)}, u32[]{:S(2)}) async-start(bf16[8,128,96]{1,2,0:T(8,128)(2,1)} %bitcast.7), calls=%async_computation.2 | async-start | bytes 393216 | tf_op jit(solution)/shard_map/all_to_all | solution.py:118
  52.2 9.9 %copy-start.40 = (f32[2,512]{1,0:T(2,128)}, f32[2,512]{1,0:T(2,128)S(1)}, u32[]{:S(2)}) copy-start(f32[2,512]{1,0:T(2,128)S(1)} %get-tuple-element.448) | copy-start | bytes 12292
  52.3 23.3 %copy-start.5 = (bf16[2,512,96]{1,2,0:T(8,128)(2,1)}, bf16[2,512,96]{1,2,0:T(8,128)(2,1)S(1)}, u32[]{:S(2)}) copy-start(bf16[2,512,96]{1,2,0:T(8,128)(2,1)S(1)} %get-tuple-element.91) | copy-start | bytes 589828
  62.1 11.1 %all-to-all-start.3 = ((bf16[8,2,6144]{2,1,0:T(2,128)(2,1)}), bf16[8,2,6144]{2,1,0:T(2,128)(2,1)S(1)}, u32[]{:S(2)}, u32[]{:S(2)}) async-start(bf16[8,2,6144]{2,1,0:T(2,128)(2,1)} %reshape.155), calls=%async_computation.3 | async-start | bytes 393216 | tf_op jit(solution)/shard_map/all_to_all | solution.py:125
  65.5 86.7 %all-reduce.6.cloned.1.call-start = ((), (), s32[]{:S(2)}) async-start(), calls=%async_computation.9 | async-start | bytes 393216 | tf_op jit(solution)/shard_map/psum | solution.py:172
  75.7 11.1 %copy-start.4 = (bf16[128,8,96]{0,2,1:T(8,128)(2,1)}, bf16[128,8,96]{0,2,1:T(8,128)(2,1)S(1)}, u32[]{:S(2)}) copy-start(bf16[128,8,96]{0,2,1:T(8,128)(2,1)S(1)} %copy.88) | copy-start | bytes 589828
  75.7 11.1 %copy-start.7 = (bf16[1,128,1536]{2,1,0:T(8,128)(2,1)S(1)}, bf16[1,128,1536]{2,1,0:T(8,128)(2,1)}, u32[]{:S(2)}) copy-start(bf16[1,128,1536]{2,1,0:T(8,128)(2,1)} %param.21) | copy-start | bytes 1179652
  75.7 11.1 %copy-start.10 = (f32[1536]{0:T(1024)S(1)}, f32[1536]{0:T(1024)}, u32[]{:S(2)}) copy-start(f32[1536]{0:T(1024)} %get-tuple-element.238) | copy-start | bytes 18436
  75.7 11.1 %copy-start.11 = (f32[1536]{0:T(1024)S(1)}, f32[1536]{0:T(1024)}, u32[]{:S(2)}) copy-start(f32[1536]{0:T(1024)} %get-tuple-element.239) | copy-start | bytes 18436
  75.7 11.1 %copy-start.12 = (f32[1536]{0:T(1024)S(1)}, f32[1536]{0:T(1024)}, u32[]{:S(2)}) copy-start(f32[1536]{0:T(1024)} %get-tuple-element.240) | copy-start | bytes 18436
  75.7 11.1 %copy-start.13 = (f32[1536]{0:T(1024)S(1)}, f32[1536]{0:T(1024)}, u32[]{:S(2)}) copy-start(f32[1536]{0:T(1024)} %get-tuple-element.241) | copy-start | bytes 18436
  75.7 11.1 %copy-start.14 = (f32[1536]{0:T(1024)S(1)}, f32[1536]{0:T(1024)}, u32[]{:S(2)}) copy-start(f32[1536]{0:T(1024)} %get-tuple-element.242) | copy-start | bytes 18436
  75.7 11.1 %copy-start.15 = (f32[1536]{0:T(1024)S(1)}, f32[1536]{0:T(1024)}, u32[]{:S(2)}) copy-start(f32[1536]{0:T(1024)} %get-tuple-element.243) | copy-start | bytes 18436
  75.7 11.1 %copy-start.16 = (f32[1536]{0:T(1024)S(1)}, f32[1536]{0:T(1024)}, u32[]{:S(2)}) copy-start(f32[1536]{0:T(1024)} %get-tuple-element.244) | copy-start | bytes 18436
  75.8 11.1 %copy-start.17 = (f32[1536]{0:T(1024)S(1)}, f32[1536]{0:T(1024)}, u32[]{:S(2)}) copy-start(f32[1536]{0:T(1024)} %get-tuple-element.245) | copy-start | bytes 18436
  75.8 11.1 %copy-start.18 = (f32[1536]{0:T(1024)S(1)}, f32[1536]{0:T(1024)}, u32[]{:S(2)}) copy-start(f32[1536]{0:T(1024)} %get-tuple-element.246) | copy-start | bytes 18436
  75.8 11.1 %copy-start.19 = (f32[1536]{0:T(1024)S(1)}, f32[1536]{0:T(1024)}, u32[]{:S(2)}) copy-start(f32[1536]{0:T(1024)} %get-tuple-element.247) | copy-start | bytes 18436
  75.8 11.1 %copy-start.20 = (f32[1536]{0:T(1024)S(1)}, f32[1536]{0:T(1024)}, u32[]{:S(2)}) copy-start(f32[1536]{0:T(1024)} %get-tuple-element.248) | copy-start | bytes 18436
  75.8 11.1 %copy-start.21 = (f32[1536]{0:T(1024)S(1)}, f32[1536]{0:T(1024)}, u32[]{:S(2)}) copy-start(f32[1536]{0:T(1024)} %get-tuple-element.249) | copy-start | bytes 18436
  75.8 11.1 %copy-start.22 = (f32[1536]{0:T(1024)S(1)}, f32[1536]{0:T(1024)}, u32[]{:S(2)}) copy-start(f32[1536]{0:T(1024)} %get-tuple-element.250) | copy-start | bytes 18436
  75.8 11.1 %copy-start.23 = (f32[1536]{0:T(1024)S(1)}, f32[1536]{0:T(1024)}, u32[]{:S(2)}) copy-start(f32[1536]{0:T(1024)} %get-tuple-element.251) | copy-start | bytes 18436
  75.8 11.1 %copy-start.24 = (f32[1536]{0:T(1024)S(1)}, f32[1536]{0:T(1024)}, u32[]{:S(2)}) copy-start(f32[1536]{0:T(1024)} %get-tuple-element.252) | copy-start | bytes 18436
  75.8 11.1 %copy-start.25 = (f32[1536]{0:T(1024)S(1)}, f32[1536]{0:T(1024)}, u32[]{:S(2)}) copy-start(f32[1536]{0:T(1024)} %get-tuple-element.253) | copy-start | bytes 18436
  75.8 11.1 %copy-start.26 = (f32[1536]{0:T(1024)S(1)}, f32[1536]{0:T(1024)}, u32[]{:S(2)}) copy-start(f32[1536]{0:T(1024)} %get-tuple-element.254) | copy-start | bytes 18436
  75.9 11.1 %copy-start.42 = (pred[128]{0:T(512)(128)(4,1)S(1)}, pred[128]{0:T(512)(128)(4,1)}, u32[]{:S(2)}) copy-start(pred[128]{0:T(512)(128)(4,1)} %add_compare_fusion) | copy-start | bytes 388
  75.9 11.1 %copy-start.44 = (f32[1536]{0:T(1024)S(1)}, f32[1536]{0:T(1024)}, u32[]{:S(2)}) copy-start(f32[1536]{0:T(1024)} %param.20) | copy-start | bytes 18436
  78.7 5.0 %collective-permute-start = (bf16[15,1536]{1,0:T(8,128)(2,1)S(1)}, bf16[15,1536]{1,0:T(8,128)(2,1)S(1)}, u32[]{:S(2)}, u32[]{:S(2)}) collective-permute-start(bf16[15,1536]{1,0:T(8,128)(2,1)S(1)} %get-tuple-element.307), channel_id=1, source_target_pairs={{0,4},{4,8},{8,12},{12,16},{16,20},{20,24},{24,28},{1,5},{5,9},{9,... | collective-permute-start | bytes 138248 | tf_op jit(solution)/shard_map/ppermute | solution.py:21
  80.7 6.0 %collective-permute-start.1 = (bf16[15,1536]{1,0:T(8,128)(2,1)S(1)}, bf16[15,1536]{1,0:T(8,128)(2,1)S(1)}, u32[]{:S(2)}, u32[]{:S(2)}) collective-permute-start(bf16[15,1536]{1,0:T(8,128)(2,1)S(1)} %get-tuple-element.308), channel_id=1, source_target_pairs={{4,0},{8,4},{12,8},{16,12},{20,16},{24,20},{28,24},{5,1},{9,5},{13... | collective-permute-start | bytes 138248 | tf_op jit(solution)/shard_map/ppermute | solution.py:22
  83.6 10.2 %copy-start.27 = (f32[1536]{0:T(1024)}, f32[1536]{0:T(1024)S(1)}, u32[]{:S(2)}) copy-start(f32[1536]{0:T(1024)S(1)} %get-tuple-element.255) | copy-start | bytes 18436
  83.6 10.2 %copy-start.28 = (f32[1536]{0:T(1024)}, f32[1536]{0:T(1024)S(1)}, u32[]{:S(2)}) copy-start(f32[1536]{0:T(1024)S(1)} %get-tuple-element.256) | copy-start | bytes 18436
  83.6 10.2 %copy-start.29 = (f32[1536]{0:T(1024)}, f32[1536]{0:T(1024)S(1)}, u32[]{:S(2)}) copy-start(f32[1536]{0:T(1024)S(1)} %get-tuple-element.257) | copy-start | bytes 18436
  83.6 10.2 %copy-start.30 = (f32[1536]{0:T(1024)}, f32[1536]{0:T(1024)S(1)}, u32[]{:S(2)}) copy-start(f32[1536]{0:T(1024)S(1)} %get-tuple-element.258) | copy-start | bytes 18436
  83.6 10.2 %copy-start.31 = (f32[1536]{0:T(1024)}, f32[1536]{0:T(1024)S(1)}, u32[]{:S(2)}) copy-start(f32[1536]{0:T(1024)S(1)} %get-tuple-element.259) | copy-start | bytes 18436
  83.6 10.2 %copy-start.32 = (f32[1536]{0:T(1024)}, f32[1536]{0:T(1024)S(1)}, u32[]{:S(2)}) copy-start(f32[1536]{0:T(1024)S(1)} %get-tuple-element.260) | copy-start | bytes 18436
  83.6 10.2 %copy-start.33 = (f32[1536]{0:T(1024)}, f32[1536]{0:T(1024)S(1)}, u32[]{:S(2)}) copy-start(f32[1536]{0:T(1024)S(1)} %get-tuple-element.261) | copy-start | bytes 18436
  83.7 10.2 %copy-start.34 = (f32[1536]{0:T(1024)}, f32[1536]{0:T(1024)S(1)}, u32[]{:S(2)}) copy-start(f32[1536]{0:T(1024)S(1)} %get-tuple-element.262) | copy-start | bytes 18436
  83.7 10.2 %copy-start.35 = (f32[1536]{0:T(1024)}, f32[1536]{0:T(1024)S(1)}, u32[]{:S(2)}) copy-start(f32[1536]{0:T(1024)S(1)} %get-tuple-element.263) | copy-start | bytes 18436
  83.7 10.2 %copy-start.36 = (f32[1536]{0:T(1024)}, f32[1536]{0:T(1024)S(1)}, u32[]{:S(2)}) copy-start(f32[1536]{0:T(1024)S(1)} %get-tuple-element.264) | copy-start | bytes 18436
  83.7 10.2 %copy-start.37 = (f32[1536]{0:T(1024)}, f32[1536]{0:T(1024)S(1)}, u32[]{:S(2)}) copy-start(f32[1536]{0:T(1024)S(1)} %get-tuple-element.265) | copy-start | bytes 18436
  83.7 10.2 %copy-start.38 = (f32[1536]{0:T(1024)}, f32[1536]{0:T(1024)S(1)}, u32[]{:S(2)}) copy-start(f32[1536]{0:T(1024)S(1)} %get-tuple-element.266) | copy-start | bytes 18436
  93.9 8.5 %copy-start.1 = (f32[128,1536]{1,0:T(8,128)}, f32[128,1536]{1,0:T(8,128)S(1)}, u32[]{:S(2)}) copy-start(f32[128,1536]{1,0:T(8,128)S(1)} %get-tuple-element.299) | copy-start | bytes 2359300
  93.9 25.3 %collective-permute-start.2 = (f32[15,1536]{1,0:T(8,128)S(1)}, f32[15,1536]{1,0:T(8,128)S(1)}, u32[]{:S(2)}, u32[]{:S(2)}) collective-permute-start(f32[15,1536]{1,0:T(8,128)S(1)} %get-tuple-element.305), channel_id=1, source_target_pairs={{4,0},{8,4},{12,8},{16,12},{20,16},{24,20},{28,24},{5,1},{9,5},{13... | collective-permute-start | bytes 276488 | tf_op jit(solution)/shard_map/ppermute | solution.py:22
  95.2 24.7 %collective-permute-start.3 = (f32[15,1536]{1,0:T(8,128)S(1)}, f32[15,1536]{1,0:T(8,128)}, u32[]{:S(2)}, u32[]{:S(2)}) collective-permute-start(f32[15,1536]{1,0:T(8,128)S(1)} %get-tuple-element.306), channel_id=1, source_target_pairs={{0,4},{4,8},{8,12},{12,16},{16,20},{20,24},{24,28},{1,5},{5,9},{9,... | collective-permute-start | bytes 276488 | tf_op jit(solution)/shard_map/ppermute | solution.py:21
  119.0 123.6 %reduce-scatter.2.cloned.1.call-start = ((), (), s32[]{:S(2)}) async-start(), calls=%async_computation.7 | async-start | bytes 5308416 | tf_op jit(solution)/shard_map/reduce_scatter | solution.py:170
  119.3 0.6 copy-start.9
  137.1 4.0 %copy-start.2 = (bf16[128,1536]{1,0:T(8,128)(2,1)}, bf16[128,1536]{1,0:T(8,128)(2,1)S(1)}, u32[]{:S(2)}) copy-start(bf16[128,1536]{1,0:T(8,128)(2,1)S(1)} %fusion.37) | copy-start | bytes 1179652
  142.3 19.8 %copy-start.41 = (f32[2,512]{1,0:T(2,128)S(1)}, f32[2,512]{1,0:T(2,128)}, u32[]{:S(2)}) copy-start(f32[2,512]{1,0:T(2,128)} %copy-done.40) | copy-start | bytes 12292
  144.1 15.4 %all-to-all-start.4 = ((bf16[8,128,96]{1,2,0:T(8,128)(2,1)}), bf16[8,128,96]{1,2,0:T(8,128)(2,1)S(1)}, u32[]{:S(2)}, u32[]{:S(2)}) async-start(bf16[8,128,96]{1,2,0:T(8,128)(2,1)} %bitcast.14), calls=%async_computation.4 | async-start | bytes 393216 | tf_op jit(solution)/shard_map/all_to_all | solution.py:157
  148.3 167.3 %all-reduce.8.cloned.1.call-start = ((), (), s32[]{:S(2)}) async-start(), calls=%async_computation.10 | async-start | bytes 393216 | tf_op jit(solution)/shard_map/psum | solution.py:172
  162.1 2.5 copy-start.8
  167.9 2.5 copy-start.8
  173.6 70.8 %copy-start.3 = (f32[128,1536]{1,0:T(8,128)S(1)}, f32[128,1536]{1,0:T(8,128)}, u32[]{:S(2)}) copy-start(f32[128,1536]{1,0:T(8,128)} %get-tuple-element.300) | copy-start | bytes 2359300
  173.6 70.8 %copy-start.6 = (bf16[128,1536]{1,0:T(8,128)(2,1)S(1)}, bf16[128,1536]{1,0:T(8,128)(2,1)}, u32[]{:S(2)}) copy-start(bf16[128,1536]{1,0:T(8,128)(2,1)} %get-tuple-element.310) | copy-start | bytes 1179652
  173.6 70.8 %copy-start.43 = (pred[128]{0:T(512)(128)(4,1)S(1)}, pred[128]{0:T(512)(128)(4,1)}, u32[]{:S(2)}) copy-start(pred[128]{0:T(512)(128)(4,1)} %add_compare_fusion) | copy-start | bytes 388
  178.2 67.3 %copy-start.39 = (f32[1536]{0:T(1024)S(1)}, f32[1536]{0:T(1024)}, u32[]{:S(2)}) copy-start(f32[1536]{0:T(1024)} %get-tuple-element.235) | copy-start | bytes 18436
  184.0 133.0 %all-to-all-start.5 = ((bf16[8,2,6144]{2,1,0:T(2,128)(2,1)}), bf16[8,2,6144]{2,1,0:T(2,128)(2,1)}, u32[]{:S(2)}, u32[]{:S(2)}) async-start(bf16[8,2,6144]{2,1,0:T(2,128)(2,1)} %reshape.157), calls=%async_computation.5 | async-start | bytes 393216 | tf_op jit(solution)/shard_map/all_to_all | solution.py:165
  188.1 161.4 %all-reduce.4.cloned.1.call-start = ((), (), s32[]{:S(2)}) async-start(), calls=%async_computation.8 | async-start | bytes 589824 | tf_op jit(solution)/shard_map/psum | solution.py:171
Sparse Core Ops, SparseCore 0:
  119.1 31.3 all-reduce.5
Sparse Core Ops, SparseCore 1:
  141.2 101.3 reduce-scatter.1
  246.2 69.4 all-reduce.7
  318.4 31.0 all-reduce.3
